TPU v7x, 32 devices: a whole 2x2x4 slice. The times are simulated.
32 devices in a mesh: dom: 8 (over z, y), sub: 4 (over x, core).
Axes of the slice: x: 2, y: 2, z: 4, core: 2. Of those that a mesh axis runs over, the one named last changes fastest.
Arguments:
- nodes: bfloat16 [16384, 128], P(('dom', 'sub')), may hold values from -6 to 6
- edges: bfloat16 [65536, 128], P(('dom', 'sub')), may hold values from -6 to 6
- senders: int32 [65536], P(('dom', 'sub')), may hold values from 0 to 895
- receivers: int32 [65536], P(('dom', 'sub')), may hold values from 0 to 511
- edge_live: int32 [65536], P(('dom', 'sub')), may hold values from 0 to 1, as said below
- outlet_flags: int32 [16384], P(('dom', 'sub')), may hold values 0 or 1
- send_rows: int32 [12288], P(('dom', 'sub')), may hold values from 0 to 511
- edge_first: float32 [3, 384, 128], replicated, may hold values from -0.3125 to 0.3125
- edge_bias: float32 [3, 128], replicated, may hold values from -3 to 3
- edge_second: float32 [3, 128, 128], replicated, may hold values from -0.5 to 0.5
- edge_offset: float32 [3, 128], replicated, may hold values from -3 to 3
- edge_gain: float32 [3, 128], replicated, may hold values from 0.25 to 1.75
- node_first: float32 [3, 256, 128], replicated, may hold values from -0.375 to 0.375
- node_bias: float32 [3, 128], replicated, may hold values from -3 to 3
- node_second: float32 [3, 128, 128], replicated, may hold values from -0.5 to 0.5
- node_offset: float32 [3, 128], replicated, may hold values from -3 to 3
- node_gain: float32 [3, 128], replicated, may hold values from 0.25 to 1.75
- outlet_map: float32 [3, 128, 128], replicated, may hold values from -0.5 to 0.5
- grad_out: float32 [16384, 128], P(('dom', 'sub')), may hold values from -6 to 6
Outputs:
- latent_out: float32 [16384, 128], P(('dom', 'sub'))
- latent_grad: float32 [16384, 128], P(('dom', 'sub'))
- edge_first_grad: float32 [3, 384, 128], replicated
- edge_bias_grad: float32 [3, 128], replicated
- edge_second_grad: float32 [3, 128, 128], replicated
- edge_offset_grad: float32 [3, 128], replicated
- edge_gain_grad: float32 [3, 128], replicated
- node_first_grad: float32 [3, 256, 128], replicated
- node_bias_grad: float32 [3, 128], replicated
- node_second_grad: float32 [3, 128, 128], replicated
- node_offset_grad: float32 [3, 128], replicated
- node_gain_grad: float32 [3, 128], replicated
- outlet_map_grad: float32 [3, 128, 128], replicated
Inputs may be any that keep to these rules, and one draw needn't show every extreme that they name: `edge_live`: on each device the live edge slots are the first ones of its 2048; each device has between a quarter and all of them live, and some device has all live. `senders`: indices below 512 name the device's own nodes; higher ones name halo rows.
All inputs are finite; a program needn't handle non-finite values. No bound on the sum of `outlet_flags` on one device may be relied on, other than what follows from the above.
Results may differ from a plain program's by a relative error of at most 0.018.
Values may be sent and summed in bfloat16 or wider, within the bound.
A program may use at most 320 MiB of HBM per device.

v0:
```python
import jax
import jax.numpy as jnp
from jax import lax
from jax.sharding import PartitionSpec as P


def passed_along(value, axis, steps):
    count = lax.axis_size(axis)
    first, last = (max(0, -steps), min(count, count - steps))
    return lax.ppermute(value, axis, [(source, source + steps) for source in range(first, last)])


def normalize(values):
    mean = jnp.mean(values, axis=-1, keepdims=True)
    centered = values - mean
    variance = jnp.mean(centered * centered, axis=-1, keepdims=True)
    return centered * lax.rsqrt(variance + 1e-05)


def layer_local(latent, edge_state, halo, layer_weights, senders, receivers, live, flags):
    (
        edge_first,
        edge_bias,
        edge_second,
        edge_offset,
        edge_gain,
        node_first,
        node_bias,
        node_second,
        node_offset,
        node_gain,
        outlet_map,
    ) = layer_weights
    own = latent.astype(jnp.bfloat16)
    extended = jnp.concatenate([own, halo], axis=0)
    joined = jnp.concatenate(
        [edge_state.astype(jnp.bfloat16), extended[senders], own[receivers]], axis=1
    )
    act_one = jax.nn.silu(
        jnp.dot(joined, edge_first.astype(jnp.bfloat16), preferred_element_type=jnp.float32)
        + edge_bias
    ).astype(jnp.bfloat16)
    pre_two = (
        jnp.dot(act_one, edge_second.astype(jnp.bfloat16), preferred_element_type=jnp.float32)
        + edge_offset
    )
    message = live[:, None] * (edge_gain * normalize(pre_two))
    new_edge = edge_state + message
    summed = jax.ops.segment_sum(message, receivers, num_segments=latent.shape[0])
    summed_half = summed.astype(jnp.bfloat16)
    node_in = jnp.concatenate([own, summed_half], axis=1)
    node_hidden = jax.nn.silu(
        jnp.dot(node_in, node_first.astype(jnp.bfloat16), preferred_element_type=jnp.float32)
        + node_bias
    ).astype(jnp.bfloat16)
    update = node_gain * normalize(
        jnp.dot(node_hidden, node_second.astype(jnp.bfloat16), preferred_element_type=jnp.float32)
        + node_offset
    )
    outlet = flags[:, None] * jnp.dot(
        summed_half, outlet_map.astype(jnp.bfloat16), preferred_element_type=jnp.float32
    )
    return (latent + update + outlet, new_edge)


def send_halo(latent, send_rows, low, high):
    sent = latent[send_rows].astype(jnp.bfloat16)
    from_lower = passed_along(sent[low : 2 * low], "sub", 1)
    from_upper = passed_along(sent[:low], "sub", -1)
    dom_lower = passed_along(sent[2 * low + high :], "dom", 1)
    dom_upper = passed_along(sent[2 * low : 2 * low + high], "dom", -1)
    return jnp.concatenate([from_lower, from_upper, dom_lower, dom_upper], axis=0)


def return_halo(halo_grad, send_rows, low, high, shape):
    back_high = passed_along(halo_grad[:low], "sub", -1)
    back_low = passed_along(halo_grad[low : 2 * low], "sub", 1)
    dom_back_high = passed_along(halo_grad[2 * low : 2 * low + high], "dom", -1)
    dom_back_low = passed_along(halo_grad[2 * low + high :], "dom", 1)
    returned = jnp.concatenate([back_low, back_high, dom_back_low, dom_back_high], axis=0).astype(
        jnp.float32
    )
    return jnp.zeros(shape, jnp.float32).at[send_rows].add(returned)


def flatten_all(grads):
    return jnp.concatenate([grad.reshape(-1) for grad in grads])


def unflatten_all(flat, shapes):
    pieces = []
    offset = 0
    for shape in shapes:
        length = 1
        for extent in shape:
            length = length * extent
        pieces.append(flat[offset : offset + length].reshape(shape))
        offset = offset + length
    return pieces


def on_device(
    nodes,
    edges,
    senders,
    receivers,
    edge_live,
    outlet_flags,
    send_rows,
    edge_first,
    edge_bias,
    edge_second,
    edge_offset,
    edge_gain,
    node_first,
    node_bias,
    node_second,
    node_offset,
    node_gain,
    outlet_map,
    grad_out,
):
    weights = (
        edge_first,
        edge_bias,
        edge_second,
        edge_offset,
        edge_gain,
        node_first,
        node_bias,
        node_second,
        node_offset,
        node_gain,
        outlet_map,
    )
    layers = edge_first.shape[0]
    low = nodes.shape[0] // 8
    high = nodes.shape[0] // 4
    live = edge_live.astype(jnp.float32)
    flags = outlet_flags.astype(jnp.float32)
    latent = nodes.astype(jnp.float32)
    edge_state = edges.astype(jnp.float32)

    def advance(latent_in, edge_in, halo, layer_weights):
        return layer_local(latent_in, edge_in, halo, layer_weights, senders, receivers, live, flags)

    saved = []
    for layer in range(layers):
        layer_weights = tuple((weight[layer] for weight in weights))
        halo = send_halo(latent, send_rows, low, high)
        (latent, edge_state), pullback = jax.vjp(advance, latent, edge_state, halo, layer_weights)
        saved.append(pullback)
    layer_shapes = [weight.shape[1:] for weight in weights]
    latent_grad = grad_out
    edge_grad = jnp.zeros_like(edge_state)
    per_layer = [None] * layers
    for layer in reversed(range(layers)):
        pullback = saved[layer]
        latent_grad, edge_grad, halo_grad, weight_grads = pullback((latent_grad, edge_grad))
        latent_grad = latent_grad + return_halo(halo_grad, send_rows, low, high, latent_grad.shape)
        flat = flatten_all(weight_grads)
        per_layer[layer] = flat
    stacked = jnp.stack(per_layer, axis=0)
    stacked = lax.psum(stacked, ("dom", "sub"))
    by_layer = [unflatten_all(stacked[layer], layer_shapes) for layer in range(layers)]
    results = [
        jnp.stack([by_layer[layer][which] for layer in range(layers)], axis=0)
        for which in range(len(weights))
    ]
    return (
        latent,
        latent_grad,
        results[0],
        results[1],
        results[2],
        results[3],
        results[4],
        results[5],
        results[6],
        results[7],
        results[8],
        results[9],
        results[10],
    )


def solution(mesh):
    placed = (
        P(("dom", "sub"), None),
        P(("dom", "sub"), None),
        P(("dom", "sub")),
        P(("dom", "sub")),
        P(("dom", "sub")),
        P(("dom", "sub")),
        P(("dom", "sub")),
        P(),
        P(),
        P(),
        P(),
        P(),
        P(),
        P(),
        P(),
        P(),
        P(),
        P(),
        P(("dom", "sub"), None),
    )
    return jax.shard_map(
        on_device,
        mesh=mesh,
        in_specs=placed,
        out_specs=(
            P(("dom", "sub"), None),
            P(("dom", "sub"), None),
            P(),
            P(),
            P(),
            P(),
            P(),
            P(),
            P(),
            P(),
            P(),
            P(),
            P(),
        ),
        check_vma=False,
    )
```

profile of v0, /device:TPU:0, one launch (start us, length us, event | category | flops | bytes accessed | tf_op | source)
XLA Modules:
  0.0 548.7 jit_solution(7893833300528265434)
XLA Ops:
  18.4 6.1 %collective-permute-start.2 = (bf16[128,128]{1,0:T(8,128)(2,1)}, bf16[128,128]{1,0:T(8,128)(2,1)}, u32[]{:S(2)}, u32[]{:S(2)}) collective-permute-start(bf16[128,128]{1,0:T(8,128)(2,1)} %get-tuple-element.114), channel_id=1, source_target_pairs={{0,4},{4,8},{8,12},{12,16},{16,20},{20,24},{24,28},{1,5},{5,9},{9,... | collective-permute-start | bytes 98312 | tf_op jit(solution)/shard_map/ppermute | solution.py:10
  33.6 6.2 %gather_fusion.2 = bf16[2048,128]{1,0:T(8,128)(2,1)S(1)} fusion(bf16[512,128]{1,0:T(8,128)(2,1)S(1)} %copy-done, s32[2048]{0:T(1024)S(1)} %get-tuple-element.118), kind=kCustom, calls=%fused_computation.2 | custom fusion | bytes 1056768 | tf_op jit(solution)/shard_map/jvp()/gather | solution.py:37
  42.0 6.2 %gather_fusion.1 = bf16[2048,128]{1,0:T(8,128)(2,1)S(1)} fusion(bf16[896,128]{1,0:T(8,128)(2,1)S(1)} %constant_dynamic-update-slice_fusion, s32[2048]{0:T(1024)S(1)} %get-tuple-element.121), kind=kCustom, calls=%fused_computation.1 | custom fusion | bytes 1056768 | tf_op jit(solution)/shard_map/jvp()/gather | solution.py:37
  53.7 11.9 %scatter_custom_fusion = f32[512,128]{1,0:T(8,128)S(1)} fusion(s32[2048]{0:T(1024)S(1)} %copy-done.84, f32[2048,128]{1,0:T(8,128)} %copy.74, f32[]{:T(128)} %constant.51.clone.1), kind=kCustom, calls=%fused_computation.256 | custom fusion | flops 262144 | bytes 262656 | tf_op jit(solution)/shard_map/jvp()/scatter-add | solution.py:49
  71.2 5.5 collective-permute-start.6
  82.0 6.2 %gather_fusion.5 = bf16[2048,128]{1,0:T(8,128)(2,1)S(1)} fusion(bf16[512,128]{1,0:T(8,128)(2,1)S(1)} %copy.80, s32[2048]{0:T(1024)S(1)} %copy-done.66), kind=kCustom, calls=%fused_computation.5 | custom fusion | bytes 1056768 | tf_op jit(solution)/shard_map/jvp()/gather | solution.py:37
  91.0 6.2 %gather_fusion.4 = bf16[2048,128]{1,0:T(8,128)(2,1)S(1)} fusion(bf16[896,128]{1,0:T(8,128)(2,1)S(1)} %copy.79, s32[2048]{0:T(1024)S(1)} %copy-done.60), kind=kCustom, calls=%fused_computation.4 | custom fusion | bytes 1056768 | tf_op jit(solution)/shard_map/jvp()/gather | solution.py:37
  106.6 11.9 %scatter_custom_fusion.1 = f32[512,128]{1,0:T(8,128)S(1)} fusion(s32[2048]{0:T(1024)S(1)} %copy-done.85, f32[2048,128]{1,0:T(8,128)} %copy.83, f32[]{:T(128)} %constant.51.clone.1), kind=kCustom, calls=%fused_computation.254 | custom fusion | flops 262144 | bytes 262656 | tf_op jit(solution)/shard_map/jvp()/scatter-add | solution.py:49
  126.5 4.4 collective-permute-start.8
  132.2 5.3 collective-permute-start.10
  137.7 7.2 %gather_fusion.8 = bf16[2048,128]{1,0:T(8,128)(2,1)S(1)} fusion(bf16[512,128]{1,0:T(8,128)(2,1)S(1)} %copy.89, s32[2048]{0:T(1024)} %copy-done.65), kind=kCustom, calls=%fused_computation.8 | custom fusion | bytes 1056768 | tf_op jit(solution)/shard_map/jvp()/gather | solution.py:37
  147.1 7.2 %gather_fusion.7 = bf16[2048,128]{1,0:T(8,128)(2,1)S(1)} fusion(bf16[896,128]{1,0:T(8,128)(2,1)S(1)} %copy.88, s32[2048]{0:T(1024)} %copy-done.59), kind=kCustom, calls=%fused_computation.7 | custom fusion | bytes 1056768 | tf_op jit(solution)/shard_map/jvp()/gather | solution.py:37
  163.6 12.9 %scatter_custom_fusion.2 = f32[512,128]{1,0:T(8,128)} fusion(s32[2048]{0:T(1024)} %param.22, f32[2048,128]{1,0:T(8,128)} %copy.92, f32[]{:T(128)} %constant.51.clone.1), kind=kCustom, calls=%fused_computation.252 | custom fusion | flops 262144 | bytes 262656 | tf_op jit(solution)/shard_map/jvp()/scatter-add | solution.py:49
  190.0 8.4 %gather_fusion.9 = f32[2048,128]{1,0:T(8,128)} fusion(f32[512,128]{1,0:T(8,128)S(1)} %fusion.19, s32[2048]{0:T(1024)} %get-tuple-element.119), kind=kCustom, calls=%fused_computation.9 | custom fusion | bytes 2105344 | tf_op jit(solution)/shard_map/transpose(jvp())/gather | solution.py:49
  212.5 11.9 %scatter_custom_fusion.3 = bf16[896,128]{1,0:T(8,128)(2,1)S(1)} fusion(s32[2048]{0:T(1024)} %get-tuple-element.120, bf16[2048,128]{1,0:T(8,128)(2,1)} %copy.99, bf16[]{:T(256)} %constant.59.clone.1), kind=kCustom, calls=%fused_computation.261 | custom fusion | flops 262144 | bytes 229888 | tf_op jit(solution)/shard_map/transpose(jvp())/scatter-add | solution.py:37
  231.6 4.6 collective-permute-start.14
  237.4 11.9 %scatter_fusion = bf16[512,128]{1,0:T(8,128)(2,1)S(1)} fusion(bf16[512,128]{1,0:T(8,128)(2,1)S(1)} %slice_add_fusion.2, s32[2048]{0:T(1024)} %get-tuple-element.117, bf16[2048,128]{1,0:T(8,128)(2,1)S(1)} %copy.100), kind=kCustom, calls=%fused_computation.16 | custom fusion | flops 262144 | bytes 1581056 | tf_op jit(solution)/shard_map/transpose(jvp())/scatter-add | solution.py:37
  279.9 7.6 %gather_fusion.10 = f32[2048,128]{1,0:T(8,128)} fusion(f32[512,128]{1,0:T(8,128)S(1)} %fusion.21, s32[2048]{0:T(1024)S(1)} %copy-done.70), kind=kCustom, calls=%fused_computation.10 | custom fusion | bytes 2105344 | tf_op jit(solution)/shard_map/transpose(jvp())/gather | solution.py:49
  301.4 11.9 %scatter_custom_fusion.6 = bf16[896,128]{1,0:T(8,128)(2,1)S(1)} fusion(s32[2048]{0:T(1024)} %get-tuple-element.120, bf16[2048,128]{1,0:T(8,128)(2,1)} %copy.105, bf16[]{:T(256)} %constant.59.clone.1), kind=kCustom, calls=%fused_computation.259 | custom fusion | flops 262144 | bytes 229888 | tf_op jit(solution)/shard_map/transpose(jvp())/scatter-add | solution.py:37
  315.9 11.8 %scatter_fusion.1 = bf16[512,128]{1,0:T(8,128)(2,1)S(1)} fusion(bf16[512,128]{1,0:T(8,128)(2,1)S(1)} %slice_add_fusion.1, s32[2048]{0:T(1024)} %get-tuple-element.117, bf16[2048,128]{1,0:T(8,128)(2,1)S(1)} %copy.106), kind=kCustom, calls=%fused_computation.19 | custom fusion | flops 262144 | bytes 1581056 | tf_op jit(solution)/shard_map/transpose(jvp())/scatter-add | solution.py:37
  368.5 8.4 %gather_fusion.11 = f32[2048,128]{1,0:T(8,128)} fusion(f32[512,128]{1,0:T(8,128)S(1)} %fusion.23, s32[2048]{0:T(1024)} %get-tuple-element.119), kind=kCustom, calls=%fused_computation.11 | custom fusion | bytes 2105344 | tf_op jit(solution)/shard_map/transpose(jvp())/gather | solution.py:49
  392.2 11.9 %scatter_custom_fusion.9 = bf16[896,128]{1,0:T(8,128)(2,1)S(1)} fusion(s32[2048]{0:T(1024)} %get-tuple-element.120, bf16[2048,384]{1,0:T(8,128)(2,1)S(1)} %convolution_convert_fusion, bf16[]{:T(256)} %constant.59.clone.1), kind=kCustom, calls=%fused_computation.171 | custom fusion | flops 262144 | bytes 754176 | tf_op jit(solution)/shard_map/transpose(jvp())/scatter-add | solution.py:37
  404.1 12.0 %scatter_custom_fusion.10 = bf16[512,128]{1,0:T(8,128)(2,1)S(1)} fusion(bf16[512,128]{1,0:T(8,128)(2,1)S(1)} %slice_add_fusion, s32[2048]{0:T(1024)} %get-tuple-element.117, bf16[2048,384]{1,0:T(8,128)(2,1)S(1)} %convolution_convert_fusion), kind=kCustom, calls=%fused_computation.169 | custom fusion | flops 262144 | bytes 655360 | tf_op jit(solution)/shard_map/transpose(jvp())/scatter-add | solution.py:37
  434.4 96.1 %all-reduce.2.cloned.1.call-done = f32[3,131840]{1,0:T(4,128)} async-done(((f32[3,131840]{1,0:T(4,128)}), f32[3,131840]{1,0:T(4,128)}) %all-reduce.2.cloned.1.call-update) | async-done | bytes 1582096 | tf_op jit(solution)/shard_map/psum | solution.py:164
  (531 shorter events, 238.3 us)
Async XLA Ops:
  7.3 523.3 %all-reduce.2.cloned.1.call-start = ((), (), s32[]{:S(2)}) async-start(), calls=%async_computation | async-start | bytes 4218880 | tf_op jit(solution)/shard_map/psum | solution.py:164
  11.4 29.1 %collective-permute-start.1 = (bf16[64,128]{1,0:T(8,128)(2,1)}, bf16[64,128]{1,0:T(8,128)(2,1)}, u32[]{:S(2)}, u32[]{:S(2)}) collective-permute-start(bf16[64,128]{1,0:T(8,128)(2,1)} %get-tuple-element.115), channel_id=1, source_target_pairs={{1,0},{2,1},{3,2},{5,4},{6,5},{7,6},{9,8},{10,9},{11,10},{13,12},{... | collective-permute-start | bytes 49160 | tf_op jit(solution)/shard_map/ppermute | solution.py:10
  12.7 27.1 %collective-permute-start = (bf16[64,128]{1,0:T(8,128)(2,1)}, bf16[64,128]{1,0:T(8,128)(2,1)}, u32[]{:S(2)}, u32[]{:S(2)}) collective-permute-start(bf16[64,128]{1,0:T(8,128)(2,1)} %get-tuple-element.116), channel_id=1, source_target_pairs={{0,1},{1,2},{2,3},{4,5},{5,6},{6,7},{8,9},{9,10},{10,11},{12,13},{... | collective-permute-start | bytes 49160 | tf_op jit(solution)/shard_map/ppermute | solution.py:10
  17.1 24.9 %collective-permute-start.3 = (bf16[128,128]{1,0:T(8,128)(2,1)}, bf16[128,128]{1,0:T(8,128)(2,1)S(1)}, u32[]{:S(2)}, u32[]{:S(2)}) collective-permute-start(bf16[128,128]{1,0:T(8,128)(2,1)} %get-tuple-element.113), channel_id=1, source_target_pairs={{4,0},{8,4},{12,8},{16,12},{20,16},{24,20},{28,24},{5,1},{9,5},{13... | collective-permute-start | bytes 98312 | tf_op jit(solution)/shard_map/ppermute | solution.py:10
  18.4 22.8 %collective-permute-start.2 = (bf16[128,128]{1,0:T(8,128)(2,1)}, bf16[128,128]{1,0:T(8,128)(2,1)}, u32[]{:S(2)}, u32[]{:S(2)}) collective-permute-start(bf16[128,128]{1,0:T(8,128)(2,1)} %get-tuple-element.114), channel_id=1, source_target_pairs={{0,4},{4,8},{8,12},{12,16},{16,20},{20,24},{24,28},{1,5},{5,9},{9,... | collective-permute-start | bytes 98312 | tf_op jit(solution)/shard_map/ppermute | solution.py:10
  69.9 19.4 %collective-permute-start.7 = (bf16[128,128]{0,1:T(8,128)(2,1)S(1)}, bf16[128,128]{0,1:T(8,128)(2,1)}, u32[]{:S(2)}, u32[]{:S(2)}) collective-permute-start(bf16[128,128]{0,1:T(8,128)(2,1)S(1)} %get-tuple-element.109), channel_id=1, source_target_pairs={{4,0},{8,4},{12,8},{16,12},{20,16},{24,20},{28,24},{5,1},{9,5},{13... | collective-permute-start | bytes 98312 | tf_op jit(solution)/shard_map/ppermute | solution.py:10
  71.2 18.7 %collective-permute-start.6 = (bf16[128,128]{0,1:T(8,128)(2,1)S(1)}, bf16[128,128]{0,1:T(8,128)(2,1)}, u32[]{:S(2)}, u32[]{:S(2)}) collective-permute-start(bf16[128,128]{0,1:T(8,128)(2,1)S(1)} %get-tuple-element.110), channel_id=1, source_target_pairs={{0,4},{4,8},{8,12},{12,16},{16,20},{20,24},{24,28},{1,5},{5,9},{9,... | collective-permute-start | bytes 98312 | tf_op jit(solution)/shard_map/ppermute | solution.py:10
  77.3 12.0 %collective-permute-start.5 = (bf16[64,128]{0,1:T(8,128)(2,1)}, bf16[64,128]{0,1:T(8,128)(2,1)S(1)}, u32[]{:S(2)}, u32[]{:S(2)}) collective-permute-start(bf16[64,128]{0,1:T(8,128)(2,1)} %get-tuple-element.111), channel_id=1, source_target_pairs={{1,0},{2,1},{3,2},{5,4},{6,5},{7,6},{9,8},{10,9},{11,10},{13,12},{... | collective-permute-start | bytes 49160 | tf_op jit(solution)/shard_map/ppermute | solution.py:10
  78.6 10.7 %collective-permute-start.4 = (bf16[64,128]{0,1:T(8,128)(2,1)S(1)}, bf16[64,128]{0,1:T(8,128)(2,1)S(1)}, u32[]{:S(2)}, u32[]{:S(2)}) collective-permute-start(bf16[64,128]{0,1:T(8,128)(2,1)S(1)} %get-tuple-element.112), channel_id=1, source_target_pairs={{0,1},{1,2},{2,3},{4,5},{5,6},{6,7},{8,9},{9,10},{10,11},{12,13},{... | collective-permute-start | bytes 49160 | tf_op jit(solution)/shard_map/ppermute | solution.py:10
  125.2 20.8 %collective-permute-start.9 = (bf16[64,128]{0,1:T(8,128)(2,1)}, bf16[64,128]{0,1:T(8,128)(2,1)}, u32[]{:S(2)}, u32[]{:S(2)}) collective-permute-start(bf16[64,128]{0,1:T(8,128)(2,1)} %get-tuple-element.107), channel_id=1, source_target_pairs={{1,0},{2,1},{3,2},{5,4},{6,5},{7,6},{9,8},{10,9},{11,10},{13,12},{... | collective-permute-start | bytes 49160 | tf_op jit(solution)/shard_map/ppermute | solution.py:10
  126.5 19.5 %collective-permute-start.8 = (bf16[64,128]{0,1:T(8,128)(2,1)}, bf16[64,128]{0,1:T(8,128)(2,1)}, u32[]{:S(2)}, u32[]{:S(2)}) collective-permute-start(bf16[64,128]{0,1:T(8,128)(2,1)} %get-tuple-element.108), channel_id=1, source_target_pairs={{0,1},{1,2},{2,3},{4,5},{5,6},{6,7},{8,9},{9,10},{10,11},{12,13},{... | collective-permute-start | bytes 49160 | tf_op jit(solution)/shard_map/ppermute | solution.py:10
  130.9 15.1 %collective-permute-start.11 = (bf16[128,128]{0,1:T(8,128)(2,1)}, bf16[128,128]{0,1:T(8,128)(2,1)}, u32[]{:S(2)}, u32[]{:S(2)}) collective-permute-start(bf16[128,128]{0,1:T(8,128)(2,1)} %get-tuple-element.105), channel_id=1, source_target_pairs={{4,0},{8,4},{12,8},{16,12},{20,16},{24,20},{28,24},{5,1},{9,5},{13... | collective-permute-start | bytes 98312 | tf_op jit(solution)/shard_map/ppermute | solution.py:10
  132.2 13.8 %collective-permute-start.10 = (bf16[128,128]{0,1:T(8,128)(2,1)}, bf16[128,128]{0,1:T(8,128)(2,1)}, u32[]{:S(2)}, u32[]{:S(2)}) collective-permute-start(bf16[128,128]{0,1:T(8,128)(2,1)} %get-tuple-element.106), channel_id=1, source_target_pairs={{0,4},{4,8},{8,12},{12,16},{16,20},{20,24},{24,28},{1,5},{5,9},{9,... | collective-permute-start | bytes 98312 | tf_op jit(solution)/shard_map/ppermute | solution.py:10
  226.9 41.0 %collective-permute-start.12 = (bf16[64,128]{1,0:T(8,128)(2,1)}, bf16[64,128]{1,0:T(8,128)(2,1)}, u32[]{:S(2)}, u32[]{:S(2)}) collective-permute-start(bf16[64,128]{1,0:T(8,128)(2,1)} %get-tuple-element.101), channel_id=1, source_target_pairs={{0,1},{1,2},{2,3},{4,5},{5,6},{6,7},{8,9},{9,10},{10,11},{12,13},{... | collective-permute-start | bytes 49160 | tf_op jit(solution)/shard_map/ppermute | solution.py:10
  230.3 37.6 %collective-permute-start.13 = (bf16[64,128]{1,0:T(8,128)(2,1)}, bf16[64,128]{1,0:T(8,128)(2,1)}, u32[]{:S(2)}, u32[]{:S(2)}) collective-permute-start(bf16[64,128]{1,0:T(8,128)(2,1)} %get-tuple-element.102), channel_id=1, source_target_pairs={{1,0},{2,1},{3,2},{5,4},{6,5},{7,6},{9,8},{10,9},{11,10},{13,12},{... | collective-permute-start | bytes 49160 | tf_op jit(solution)/shard_map/ppermute | solution.py:10
  231.6 36.3 %collective-permute-start.14 = (bf16[128,128]{1,0:T(8,128)(2,1)}, bf16[128,128]{1,0:T(8,128)(2,1)}, u32[]{:S(2)}, u32[]{:S(2)}) collective-permute-start(bf16[128,128]{1,0:T(8,128)(2,1)} %get-tuple-element.103), channel_id=1, source_target_pairs={{0,4},{4,8},{8,12},{12,16},{16,20},{20,24},{24,28},{1,5},{5,9},{9,... | collective-permute-start | bytes 98312 | tf_op jit(solution)/shard_map/ppermute | solution.py:10
  236.1 31.8 %collective-permute-start.15 = (bf16[128,128]{1,0:T(8,128)(2,1)}, bf16[128,128]{1,0:T(8,128)(2,1)}, u32[]{:S(2)}, u32[]{:S(2)}) collective-permute-start(bf16[128,128]{1,0:T(8,128)(2,1)} %get-tuple-element.104), channel_id=1, source_target_pairs={{4,0},{8,4},{12,8},{16,12},{20,16},{24,20},{28,24},{5,1},{9,5},{13... | collective-permute-start | bytes 98312 | tf_op jit(solution)/shard_map/ppermute | solution.py:10
  328.7 27.4 %collective-permute-start.16 = (bf16[64,128]{1,0:T(8,128)(2,1)}, bf16[64,128]{1,0:T(8,128)(2,1)S(1)}, u32[]{:S(2)}, u32[]{:S(2)}) collective-permute-start(bf16[64,128]{1,0:T(8,128)(2,1)} %get-tuple-element.97), channel_id=1, source_target_pairs={{0,1},{1,2},{2,3},{4,5},{5,6},{6,7},{8,9},{9,10},{10,11},{12,13},{... | collective-permute-start | bytes 49160 | tf_op jit(solution)/shard_map/ppermute | solution.py:10
  331.5 24.7 %collective-permute-start.17 = (bf16[64,128]{1,0:T(8,128)(2,1)}, bf16[64,128]{1,0:T(8,128)(2,1)S(1)}, u32[]{:S(2)}, u32[]{:S(2)}) collective-permute-start(bf16[64,128]{1,0:T(8,128)(2,1)} %get-tuple-element.98), channel_id=1, source_target_pairs={{1,0},{2,1},{3,2},{5,4},{6,5},{7,6},{9,8},{10,9},{11,10},{13,12},{... | collective-permute-start | bytes 49160 | tf_op jit(solution)/shard_map/ppermute | solution.py:10
  332.8 23.4 %collective-permute-start.18 = (bf16[128,128]{1,0:T(8,128)(2,1)}, bf16[128,128]{1,0:T(8,128)(2,1)S(1)}, u32[]{:S(2)}, u32[]{:S(2)}) collective-permute-start(bf16[128,128]{1,0:T(8,128)(2,1)} %get-tuple-element.99), channel_id=1, source_target_pairs={{0,4},{4,8},{8,12},{12,16},{16,20},{20,24},{24,28},{1,5},{5,9},{9,... | collective-permute-start | bytes 98312 | tf_op jit(solution)/shard_map/ppermute | solution.py:10
  337.1 19.1 %collective-permute-start.19 = (bf16[128,128]{1,0:T(8,128)(2,1)}, bf16[128,128]{1,0:T(8,128)(2,1)S(1)}, u32[]{:S(2)}, u32[]{:S(2)}) collective-permute-start(bf16[128,128]{1,0:T(8,128)(2,1)} %get-tuple-element.100), channel_id=1, source_target_pairs={{4,0},{8,4},{12,8},{16,12},{20,16},{24,20},{28,24},{5,1},{9,5},{13... | collective-permute-start | bytes 98312 | tf_op jit(solution)/shard_map/ppermute | solution.py:10
  416.1 11.0 %collective-permute-start.20 = (bf16[64,128]{1,0:T(8,128)(2,1)S(1)}, bf16[64,128]{1,0:T(8,128)(2,1)S(1)}, u32[]{:S(2)}, u32[]{:S(2)}) collective-permute-start(bf16[64,128]{1,0:T(8,128)(2,1)S(1)} %get-tuple-element.93), channel_id=1, source_target_pairs={{0,1},{1,2},{2,3},{4,5},{5,6},{6,7},{8,9},{9,10},{10,11},{12,13},{... | collective-permute-start | bytes 49160 | tf_op jit(solution)/shard_map/ppermute | solution.py:10
  420.1 6.9 %collective-permute-start.21 = (bf16[64,128]{1,0:T(8,128)(2,1)S(1)}, bf16[64,128]{1,0:T(8,128)(2,1)S(1)}, u32[]{:S(2)}, u32[]{:S(2)}) collective-permute-start(bf16[64,128]{1,0:T(8,128)(2,1)S(1)} %get-tuple-element.94), channel_id=1, source_target_pairs={{1,0},{2,1},{3,2},{5,4},{6,5},{7,6},{9,8},{10,9},{11,10},{13,12},{... | collective-permute-start | bytes 49160 | tf_op jit(solution)/shard_map/ppermute | solution.py:10
  421.4 5.9 %collective-permute-start.22 = (bf16[128,128]{1,0:T(8,128)(2,1)S(1)}, bf16[128,128]{1,0:T(8,128)(2,1)S(1)}, u32[]{:S(2)}, u32[]{:S(2)}) collective-permute-start(bf16[128,128]{1,0:T(8,128)(2,1)S(1)} %get-tuple-element.95), channel_id=1, source_target_pairs={{0,4},{4,8},{8,12},{12,16},{16,20},{20,24},{24,28},{1,5},{5,9},{9,... | collective-permute-start | bytes 98312 | tf_op jit(solution)/shard_map/ppermute | solution.py:10
  (132 other events, 1219.4 us)
Sparse Core Ops, SparseCore 0:
  392.3 138.2 all-reduce.1
where the time goes:
time: 559 us; the launch traced here: 549 us
  local copies, waits for them, and re-layouts  161 us (29%)
  other arithmetic  151 us (27%)
  waiting for transfers between devices  101 us (18%)
  starting transfers between devices  67.2 us (12%)
  matrix products  52.3 us (9%)
  between operations  16.9 us (3%)
    psum x1, waiting for transfers between devices, on_device(): stacked = lax.psum(stacked, ('dom', 'sub'))  96.1 us
    ppermute x24, starting transfers between devices, passed_along(): lax.ppermute(value, axis, [(source, source + steps) for source in range(f...  67.2 us
    scatter-add x3, other arithmetic, layer_local(): jax.ops.segment_sum(message, receivers, num_segments=latent.shape[0])  36.7 us
    unnamed x299, local copies, waits for them, and re-layouts  36.6 us
    scatter-add x3, other arithmetic, layer_local(): extended[senders]  35.8 us
    scatter-add x3, other arithmetic, layer_local(): own[receivers]  35.6 us
    gather x6, local copies, waits for them, and re-layouts, layer_local(): jax.ops.segment_sum(message, receivers, num_segments=latent.shape[0])  31 us
    gather x5, local copies, waits for them, and re-layouts, layer_local(): extended[senders]  21.6 us
  transfers between devices with their start and end apart: 25, of which 3 were waited for; matrix products, arithmetic and copies ran while one was open for 20% of the time, Pallas kernels for 0%

commit v1 on v0

--- a/solution.py
+++ b/solution.py
@@ -161,7 +161,7 @@
         flat = flatten_all(weight_grads)
         per_layer[layer] = flat
     stacked = jnp.stack(per_layer, axis=0)
-    stacked = lax.psum(stacked, ("dom", "sub"))
+    stacked = lax.all_gather(stacked, ("dom", "sub")).sum(axis=0)
     by_layer = [unflatten_all(stacked[layer], layer_shapes) for layer in range(layers)]
     results = [
         jnp.stack([by_layer[layer][which] for layer in range(layers)], axis=0)

time: 559 us -> 803 us (1.44)
  waiting for transfers between devices: 101 us -> 316 us
  other arithmetic: 151 us -> 174 us
    all_gather x0 -> x1, waiting for transfers between devices: none -> 316 us  [on_device(): stacked = lax.all_gather(stacked, ('dom', 'sub')).sum(axis=0)]
    psum x1 -> x0, waiting for transfers between devices: 96.1 us -> none  [on_device(): stacked = lax.psum(stacked, ('dom', 'sub'))]
    reduce_sum x0 -> x1, other arithmetic: none -> 21.7 us  [on_device(): stacked = lax.all_gather(stacked, ('dom', 'sub')).sum(axis=0)]
    unnamed x299 -> x377, local copies, waits for them, and re-layouts: 36.6 us -> 39.5 us
  transfers between devices with their start and end apart: 25 -> 25, of which waited for: 3 -> 1; matrix products, arithmetic and copies ran while one was open for 20% -> 13% of each run, Pallas kernels for 0% -> 0%
where the time goes in v1:
time: 803 us; the launch traced here: 792 us
  waiting for transfers between devices  316 us (39%)
  other arithmetic  174 us (22%)
  local copies, waits for them, and re-layouts  162 us (20%)
  starting transfers between devices  71 us (9%)
  matrix products  52.4 us (7%)
  between operations  17.3 us (2%)
    all_gather x1, waiting for transfers between devices, on_device(): stacked = lax.all_gather(stacked, ('dom', 'sub')).sum(axis=0)  316 us
    ppermute x24, starting transfers between devices, passed_along(): lax.ppermute(value, axis, [(source, source + steps) for source in range(f...  70.9 us
    unnamed x377, local copies, waits for them, and re-layouts  39.5 us
    scatter-add x3, other arithmetic, layer_local(): jax.ops.segment_sum(message, receivers, num_segments=latent.shape[0])  36.7 us
    scatter-add x3, other arithmetic, layer_local(): extended[senders]  35.6 us
    scatter-add x3, other arithmetic, layer_local(): own[receivers]  35.6 us
    gather x6, local copies, waits for them, and re-layouts, layer_local(): jax.ops.segment_sum(message, receivers, num_segments=latent.shape[0])  31.6 us
    gather x5, local copies, waits for them, and re-layouts, layer_local(): extended[senders]  22.5 us
  transfers between devices with their start and end apart: 25, of which 1 were waited for; matrix products, arithmetic and copies ran while one was open for 13% of the time, Pallas kernels for 0%

profile of v1, /device:TPU:0, one launch (start us, length us, event | category | flops | bytes accessed | tf_op | source)
XLA Modules:
  0.0 792.1 jit_solution(8090417507786891548)
XLA Ops:
  29.4 6.2 gather_fusion.2
  42.5 7.2 gather_fusion.1
  55.1 11.9 %scatter_custom_fusion = f32[512,128]{1,0:T(8,128)S(1)} fusion(s32[2048]{0:T(1024)} %param.22, f32[2048,128]{1,0:T(8,128)} %copy.116, f32[]{:T(128)} %constant.51.clone.1), kind=kCustom, calls=%fused_computation.256 | custom fusion | flops 262144 | bytes 262656 | tf_op jit(solution)/shard_map/jvp()/scatter-add | solution.py:49
  83.0 6.2 gather_fusion.5
  91.9 6.2 gather_fusion.4
  107.5 11.9 %scatter_custom_fusion.1 = f32[512,128]{1,0:T(8,128)S(1)} fusion(s32[2048]{0:T(1024)S(1)} %copy-done.109, f32[2048,128]{1,0:T(8,128)} %copy.125, f32[]{:T(128)} %constant.51.clone.1), kind=kCustom, calls=%fused_computation.254 | custom fusion | flops 262144 | bytes 262656 | tf_op jit(solution)/shard_map/jvp()/scatter-add | solution.py:49
  126.1 5.7 collective-permute-start.8
  139.8 7.2 gather_fusion.8
  149.1 7.2 gather_fusion.7
  165.8 12.9 %scatter_custom_fusion.2 = f32[512,128]{1,0:T(8,128)} fusion(s32[2048]{0:T(1024)} %param.22, f32[2048,128]{1,0:T(8,128)} %copy.134, f32[]{:T(128)} %constant.51.clone.1), kind=kCustom, calls=%fused_computation.252 | custom fusion | flops 262144 | bytes 262656 | tf_op jit(solution)/shard_map/jvp()/scatter-add | solution.py:49
  188.7 8.3 %gather_fusion.9 = f32[2048,128]{1,0:T(8,128)} fusion(f32[512,128]{1,0:T(8,128)S(1)} %fusion.19, s32[2048]{0:T(1024)} %get-tuple-element.132), kind=kCustom, calls=%fused_computation.9 | custom fusion | bytes 2105344 | tf_op jit(solution)/shard_map/transpose(jvp())/gather | solution.py:49
  208.8 11.9 %scatter_custom_fusion.3 = bf16[896,128]{1,0:T(8,128)(2,1)S(1)} fusion(s32[2048]{0:T(1024)} %get-tuple-element.133, bf16[2048,128]{1,0:T(8,128)(2,1)} %copy.141, bf16[]{:T(256)} %constant.59.clone.1), kind=kCustom, calls=%fused_computation.261 | custom fusion | flops 262144 | bytes 229888 | tf_op jit(solution)/shard_map/transpose(jvp())/scatter-add | solution.py:37
  230.9 11.6 %scatter_fusion = bf16[512,128]{1,0:T(8,128)(2,1)S(1)} fusion(bf16[512,128]{1,0:T(8,128)(2,1)S(1)} %slice_add_fusion.2, s32[2048]{0:T(1024)S(1)} %copy-done.83, bf16[2048,128]{1,0:T(8,128)(2,1)S(1)} %copy.142), kind=kCustom, calls=%fused_computation.16 | custom fusion | flops 262144 | bytes 1581056 | tf_op jit(solution)/shard_map/transpose(jvp())/scatter-add | solution.py:37
  244.1 5.2 collective-permute-start.14
  279.7 8.3 %gather_fusion.10 = f32[2048,128]{1,0:T(8,128)} fusion(f32[512,128]{1,0:T(8,128)S(1)} %fusion.21, s32[2048]{0:T(1024)} %get-tuple-element.132), kind=kCustom, calls=%fused_computation.10 | custom fusion | bytes 2105344 | tf_op jit(solution)/shard_map/transpose(jvp())/gather | solution.py:49
  298.7 11.9 %scatter_custom_fusion.6 = bf16[896,128]{1,0:T(8,128)(2,1)S(1)} fusion(s32[2048]{0:T(1024)} %get-tuple-element.133, bf16[2048,128]{1,0:T(8,128)(2,1)} %copy.147, bf16[]{:T(256)} %constant.59.clone.1), kind=kCustom, calls=%fused_computation.259 | custom fusion | flops 262144 | bytes 229888 | tf_op jit(solution)/shard_map/transpose(jvp())/scatter-add | solution.py:37
  321.8 12.0 %scatter_fusion.1 = bf16[512,128]{1,0:T(8,128)(2,1)S(1)} fusion(bf16[512,128]{1,0:T(8,128)(2,1)S(1)} %slice_add_fusion.1, s32[2048]{0:T(1024)S(1)} %copy-done.84, bf16[2048,128]{1,0:T(8,128)(2,1)} %copy.148), kind=kCustom, calls=%fused_computation.19 | custom fusion | flops 262144 | bytes 1581056 | tf_op jit(solution)/shard_map/transpose(jvp())/scatter-add | solution.py:37
  342.4 5.3 collective-permute-start.16
  375.5 8.3 %gather_fusion.11 = f32[2048,128]{1,0:T(8,128)} fusion(f32[512,128]{1,0:T(8,128)S(1)} %fusion.23, s32[2048]{0:T(1024)} %get-tuple-element.132), kind=kCustom, calls=%fused_computation.11 | custom fusion | bytes 2105344 | tf_op jit(solution)/shard_map/transpose(jvp())/gather | solution.py:49
  403.1 11.7 %scatter_custom_fusion.9 = bf16[896,128]{1,0:T(8,128)(2,1)S(1)} fusion(s32[2048]{0:T(1024)} %get-tuple-element.133, bf16[2048,384]{1,0:T(8,128)(2,1)S(1)} %convolution_convert_fusion, bf16[]{:T(256)} %constant.59.clone.1), kind=kCustom, calls=%fused_computation.171 | custom fusion | flops 262144 | bytes 754176 | tf_op jit(solution)/shard_map/transpose(jvp())/scatter-add | solution.py:37
  414.9 12.0 %scatter_custom_fusion.10 = bf16[512,128]{1,0:T(8,128)(2,1)S(1)} fusion(bf16[512,128]{1,0:T(8,128)(2,1)S(1)} %slice_add_fusion, s32[2048]{0:T(1024)} %get-tuple-element.130, bf16[2048,384]{1,0:T(8,128)(2,1)S(1)} %convolution_convert_fusion), kind=kCustom, calls=%fused_computation.169 | custom fusion | flops 262144 | bytes 655360 | tf_op jit(solution)/shard_map/transpose(jvp())/scatter-add | solution.py:37
  428.2 5.2 collective-permute-start.22
  442.6 315.8 %all-gather.4.cloned.1.call-done = f32[32,3,131840]{2,1,0:T(4,128)} async-done(((f32[1,3,131840]{2,1,0:T(4,128)}), f32[32,3,131840]{2,1,0:T(4,128)}) %all-gather.4.cloned.1.call-update) | async-done | bytes 50626576 | tf_op jit(solution)/shard_map/all_gather | solution.py:164
  758.4 21.7 %reduce_sum.449 = f32[3,131840]{1,0:T(4,128)S(1)} reduce(f32[32,3,131840]{2,1,0:T(4,128)} %all-gather.4.cloned.1.call-done, f32[]{:T(128)} %constant.51.clone.1), dimensions={0}, to_apply=%region_54.55 | reduce | flops 12261120 | bytes 52208644 | tf_op jit(solution)/shard_map/reduce_sum | solution.py:164
  (610 shorter events, 243.2 us)
Async XLA Ops:
  7.3 751.1 %all-gather.4.cloned.1.call-start = ((), (), s32[]{:S(2)}) async-start(), calls=%async_computation | async-start | bytes 69611520 | tf_op jit(solution)/shard_map/all_gather | solution.py:164
  12.0 27.5 %collective-permute-start = (bf16[64,128]{1,0:T(8,128)(2,1)}, bf16[64,128]{1,0:T(8,128)(2,1)}, u32[]{:S(2)}, u32[]{:S(2)}) collective-permute-start(bf16[64,128]{1,0:T(8,128)(2,1)} %get-tuple-element.129), channel_id=1, source_target_pairs={{0,1},{1,2},{2,3},{4,5},{5,6},{6,7},{8,9},{9,10},{10,11},{12,13},{... | collective-permute-start | bytes 49160 | tf_op jit(solution)/shard_map/ppermute | solution.py:10
  15.0 25.2 %collective-permute-start.1 = (bf16[64,128]{1,0:T(8,128)(2,1)}, bf16[64,128]{1,0:T(8,128)(2,1)}, u32[]{:S(2)}, u32[]{:S(2)}) collective-permute-start(bf16[64,128]{1,0:T(8,128)(2,1)} %get-tuple-element.128), channel_id=1, source_target_pairs={{1,0},{2,1},{3,2},{5,4},{6,5},{7,6},{9,8},{10,9},{11,10},{13,12},{... | collective-permute-start | bytes 49160 | tf_op jit(solution)/shard_map/ppermute | solution.py:10
  16.9 24.0 %collective-permute-start.2 = (bf16[128,128]{1,0:T(8,128)(2,1)}, bf16[128,128]{1,0:T(8,128)(2,1)}, u32[]{:S(2)}, u32[]{:S(2)}) collective-permute-start(bf16[128,128]{1,0:T(8,128)(2,1)} %get-tuple-element.127), channel_id=1, source_target_pairs={{0,4},{4,8},{8,12},{12,16},{16,20},{20,24},{24,28},{1,5},{5,9},{9,... | collective-permute-start | bytes 98312 | tf_op jit(solution)/shard_map/ppermute | solution.py:10
  21.7 20.0 %collective-permute-start.3 = (bf16[128,128]{1,0:T(8,128)(2,1)}, bf16[128,128]{1,0:T(8,128)(2,1)}, u32[]{:S(2)}, u32[]{:S(2)}) collective-permute-start(bf16[128,128]{1,0:T(8,128)(2,1)} %get-tuple-element.126), channel_id=1, source_target_pairs={{4,0},{8,4},{12,8},{16,12},{20,16},{24,20},{28,24},{5,1},{9,5},{13... | collective-permute-start | bytes 98312 | tf_op jit(solution)/shard_map/ppermute | solution.py:10
  71.3 18.9 %collective-permute-start.6 = (bf16[128,128]{0,1:T(8,128)(2,1)S(1)}, bf16[128,128]{0,1:T(8,128)(2,1)}, u32[]{:S(2)}, u32[]{:S(2)}) collective-permute-start(bf16[128,128]{0,1:T(8,128)(2,1)S(1)} %get-tuple-element.123), channel_id=1, source_target_pairs={{0,4},{4,8},{8,12},{12,16},{16,20},{20,24},{24,28},{1,5},{5,9},{9,... | collective-permute-start | bytes 98312 | tf_op jit(solution)/shard_map/ppermute | solution.py:10
  76.4 14.4 %collective-permute-start.7 = (bf16[128,128]{0,1:T(8,128)(2,1)S(1)}, bf16[128,128]{0,1:T(8,128)(2,1)}, u32[]{:S(2)}, u32[]{:S(2)}) collective-permute-start(bf16[128,128]{0,1:T(8,128)(2,1)S(1)} %get-tuple-element.122), channel_id=1, source_target_pairs={{4,0},{8,4},{12,8},{16,12},{20,16},{24,20},{28,24},{5,1},{9,5},{13... | collective-permute-start | bytes 98312 | tf_op jit(solution)/shard_map/ppermute | solution.py:10
  78.4 11.8 %collective-permute-start.4 = (bf16[64,128]{0,1:T(8,128)(2,1)}, bf16[64,128]{0,1:T(8,128)(2,1)S(1)}, u32[]{:S(2)}, u32[]{:S(2)}) collective-permute-start(bf16[64,128]{0,1:T(8,128)(2,1)} %get-tuple-element.125), channel_id=1, source_target_pairs={{0,1},{1,2},{2,3},{4,5},{5,6},{6,7},{8,9},{9,10},{10,11},{12,13},{... | collective-permute-start | bytes 49160 | tf_op jit(solution)/shard_map/ppermute | solution.py:10
  81.3 8.9 %collective-permute-start.5 = (bf16[64,128]{0,1:T(8,128)(2,1)S(1)}, bf16[64,128]{0,1:T(8,128)(2,1)S(1)}, u32[]{:S(2)}, u32[]{:S(2)}) collective-permute-start(bf16[64,128]{0,1:T(8,128)(2,1)S(1)} %get-tuple-element.124), channel_id=1, source_target_pairs={{1,0},{2,1},{3,2},{5,4},{6,5},{7,6},{9,8},{10,9},{11,10},{13,12},{... | collective-permute-start | bytes 49160 | tf_op jit(solution)/shard_map/ppermute | solution.py:10
  126.1 21.9 %collective-permute-start.8 = (bf16[64,128]{0,1:T(8,128)(2,1)}, bf16[64,128]{0,1:T(8,128)(2,1)}, u32[]{:S(2)}, u32[]{:S(2)}) collective-permute-start(bf16[64,128]{0,1:T(8,128)(2,1)} %get-tuple-element.121), channel_id=1, source_target_pairs={{0,1},{1,2},{2,3},{4,5},{5,6},{6,7},{8,9},{9,10},{10,11},{12,13},{... | collective-permute-start | bytes 49160 | tf_op jit(solution)/shard_map/ppermute | solution.py:10
  131.8 16.2 %collective-permute-start.9 = (bf16[64,128]{0,1:T(8,128)(2,1)}, bf16[64,128]{0,1:T(8,128)(2,1)}, u32[]{:S(2)}, u32[]{:S(2)}) collective-permute-start(bf16[64,128]{0,1:T(8,128)(2,1)} %get-tuple-element.120), channel_id=1, source_target_pairs={{1,0},{2,1},{3,2},{5,4},{6,5},{7,6},{9,8},{10,9},{11,10},{13,12},{... | collective-permute-start | bytes 49160 | tf_op jit(solution)/shard_map/ppermute | solution.py:10
  133.1 14.9 %collective-permute-start.10 = (bf16[128,128]{0,1:T(8,128)(2,1)}, bf16[128,128]{0,1:T(8,128)(2,1)}, u32[]{:S(2)}, u32[]{:S(2)}) collective-permute-start(bf16[128,128]{0,1:T(8,128)(2,1)} %get-tuple-element.119), channel_id=1, source_target_pairs={{0,4},{4,8},{8,12},{12,16},{16,20},{20,24},{24,28},{1,5},{5,9},{9,... | collective-permute-start | bytes 98312 | tf_op jit(solution)/shard_map/ppermute | solution.py:10
  138.2 9.8 %collective-permute-start.11 = (bf16[128,128]{0,1:T(8,128)(2,1)}, bf16[128,128]{0,1:T(8,128)(2,1)}, u32[]{:S(2)}, u32[]{:S(2)}) collective-permute-start(bf16[128,128]{0,1:T(8,128)(2,1)} %get-tuple-element.118), channel_id=1, source_target_pairs={{4,0},{8,4},{12,8},{16,12},{20,16},{24,20},{28,24},{5,1},{9,5},{13... | collective-permute-start | bytes 98312 | tf_op jit(solution)/shard_map/ppermute | solution.py:10
  242.6 29.0 %collective-permute-start.15 = (bf16[128,128]{1,0:T(8,128)(2,1)}, bf16[128,128]{1,0:T(8,128)(2,1)S(1)}, u32[]{:S(2)}, u32[]{:S(2)}) collective-permute-start(bf16[128,128]{1,0:T(8,128)(2,1)} %get-tuple-element.117), channel_id=1, source_target_pairs={{4,0},{8,4},{12,8},{16,12},{20,16},{24,20},{28,24},{5,1},{9,5},{13... | collective-permute-start | bytes 98312 | tf_op jit(solution)/shard_map/ppermute | solution.py:10
  244.1 27.5 %collective-permute-start.14 = (bf16[128,128]{1,0:T(8,128)(2,1)S(1)}, bf16[128,128]{1,0:T(8,128)(2,1)S(1)}, u32[]{:S(2)}, u32[]{:S(2)}) collective-permute-start(bf16[128,128]{1,0:T(8,128)(2,1)S(1)} %copy-done.111), channel_id=1, source_target_pairs={{0,4},{4,8},{8,12},{12,16},{16,20},{20,24},{24,28},{1,5},{5,9},{9,... | collective-permute-start | bytes 98312 | tf_op jit(solution)/shard_map/ppermute | solution.py:10
  249.3 22.3 %collective-permute-start.13 = (bf16[64,128]{1,0:T(8,128)(2,1)}, bf16[64,128]{1,0:T(8,128)(2,1)S(1)}, u32[]{:S(2)}, u32[]{:S(2)}) collective-permute-start(bf16[64,128]{1,0:T(8,128)(2,1)} %get-tuple-element.115), channel_id=1, source_target_pairs={{1,0},{2,1},{3,2},{5,4},{6,5},{7,6},{9,8},{10,9},{11,10},{13,12},{... | collective-permute-start | bytes 49160 | tf_op jit(solution)/shard_map/ppermute | solution.py:10
  250.6 21.0 %collective-permute-start.12 = (bf16[64,128]{1,0:T(8,128)(2,1)}, bf16[64,128]{1,0:T(8,128)(2,1)S(1)}, u32[]{:S(2)}, u32[]{:S(2)}) collective-permute-start(bf16[64,128]{1,0:T(8,128)(2,1)} %get-tuple-element.114), channel_id=1, source_target_pairs={{0,1},{1,2},{2,3},{4,5},{5,6},{6,7},{8,9},{9,10},{10,11},{12,13},{... | collective-permute-start | bytes 49160 | tf_op jit(solution)/shard_map/ppermute | solution.py:10
  334.5 30.9 %collective-permute-start.19 = (bf16[128,128]{1,0:T(8,128)(2,1)}, bf16[128,128]{1,0:T(8,128)(2,1)S(1)}, u32[]{:S(2)}, u32[]{:S(2)}) collective-permute-start(bf16[128,128]{1,0:T(8,128)(2,1)} %get-tuple-element.113), channel_id=1, source_target_pairs={{4,0},{8,4},{12,8},{16,12},{20,16},{24,20},{28,24},{5,1},{9,5},{13... | collective-permute-start | bytes 98312 | tf_op jit(solution)/shard_map/ppermute | solution.py:10
  335.9 29.4 %collective-permute-start.18 = (bf16[128,128]{1,0:T(8,128)(2,1)S(1)}, bf16[128,128]{1,0:T(8,128)(2,1)S(1)}, u32[]{:S(2)}, u32[]{:S(2)}) collective-permute-start(bf16[128,128]{1,0:T(8,128)(2,1)S(1)} %copy-done.110), channel_id=1, source_target_pairs={{0,4},{4,8},{8,12},{12,16},{16,20},{20,24},{24,28},{1,5},{5,9},{9,... | collective-permute-start | bytes 98312 | tf_op jit(solution)/shard_map/ppermute | solution.py:10
  341.1 24.2 %collective-permute-start.17 = (bf16[64,128]{1,0:T(8,128)(2,1)}, bf16[64,128]{1,0:T(8,128)(2,1)S(1)}, u32[]{:S(2)}, u32[]{:S(2)}) collective-permute-start(bf16[64,128]{1,0:T(8,128)(2,1)} %get-tuple-element.111), channel_id=1, source_target_pairs={{1,0},{2,1},{3,2},{5,4},{6,5},{7,6},{9,8},{10,9},{11,10},{13,12},{... | collective-permute-start | bytes 49160 | tf_op jit(solution)/shard_map/ppermute | solution.py:10
  342.4 22.9 %collective-permute-start.16 = (bf16[64,128]{1,0:T(8,128)(2,1)}, bf16[64,128]{1,0:T(8,128)(2,1)S(1)}, u32[]{:S(2)}, u32[]{:S(2)}) collective-permute-start(bf16[64,128]{1,0:T(8,128)(2,1)} %get-tuple-element.110), channel_id=1, source_target_pairs={{0,1},{1,2},{2,3},{4,5},{5,6},{6,7},{8,9},{9,10},{10,11},{12,13},{... | collective-permute-start | bytes 49160 | tf_op jit(solution)/shard_map/ppermute | solution.py:10
  426.9 12.8 %collective-permute-start.23 = (bf16[128,128]{1,0:T(8,128)(2,1)S(1)}, bf16[128,128]{1,0:T(8,128)(2,1)S(1)}, u32[]{:S(2)}, u32[]{:S(2)}) collective-permute-start(bf16[128,128]{1,0:T(8,128)(2,1)S(1)} %get-tuple-element.109), channel_id=1, source_target_pairs={{4,0},{8,4},{12,8},{16,12},{20,16},{24,20},{28,24},{5,1},{9,5},{13... | collective-permute-start | bytes 98312 | tf_op jit(solution)/shard_map/ppermute | solution.py:10
  428.2 11.5 %collective-permute-start.22 = (bf16[128,128]{1,0:T(8,128)(2,1)S(1)}, bf16[128,128]{1,0:T(8,128)(2,1)S(1)}, u32[]{:S(2)}, u32[]{:S(2)}) collective-permute-start(bf16[128,128]{1,0:T(8,128)(2,1)S(1)} %get-tuple-element.108), channel_id=1, source_target_pairs={{0,4},{4,8},{8,12},{12,16},{16,20},{20,24},{24,28},{1,5},{5,9},{9,... | collective-permute-start | bytes 98312 | tf_op jit(solution)/shard_map/ppermute | solution.py:10
  433.4 6.3 collective-permute-start.21
  (171 other events, 1724.4 us)
Sparse Core Ops, SparseCore 0:
  398.9 359.4 all-gather.3
